TPU v7x, 32 devices: a whole 2x2x4 slice. The times are simulated.
32 devices in a mesh: fsdp: 8 (over z, core), tp: 4 (over y, x).
Axes of the slice: x: 2, y: 2, z: 4, core: 2. Of those that a mesh axis runs over, the one named last changes fastest.
Arguments:
- layer_input: bfloat16 [8192, 2048], P(('fsdp', 'tp')), may hold values from -6 to 6
- cotangent: bfloat16 [8192, 2048], P(('fsdp', 'tp')), may hold values from -6 to 6
- segment_ids: int32 [8192], P('fsdp'), may hold values from 0 to 12, as said below
- path_positions: int32 [8192], P('fsdp'), may hold values from 0 to 383, as said below
- ancestor_masks: int32 [8, 13, 13], P('fsdp'), may hold values from 0 to 1, as said below
- attn_gain: bfloat16 [2048], P('fsdp'), may hold values from 0.5 to 1.5
- query_weight: bfloat16 [2048, 2048], P('fsdp', 'tp'), may hold values from -0.125 to 0.125
- key_weight: bfloat16 [2048, 512], P('fsdp', 'tp'), may hold values from -0.125 to 0.125
- value_weight: bfloat16 [2048, 512], P('fsdp', 'tp'), may hold values from -0.125 to 0.125
- out_weight: bfloat16 [2048, 2048], P('tp', 'fsdp'), may hold values from -1.5 to 1.5
- mlp_gain: bfloat16 [2048], P('fsdp'), may hold values from 0.5 to 1.5
- gate_weight: bfloat16 [2048, 8192], P('fsdp', 'tp'), may hold values from -0.125 to 0.125
- up_weight: bfloat16 [2048, 8192], P('fsdp', 'tp'), may hold values from -0.125 to 0.125
- down_weight: bfloat16 [8192, 2048], P('tp', 'fsdp'), may hold values from -0.0625 to 0.0625
Outputs:
- output: bfloat16 [8192, 2048], P(('fsdp', 'tp'))
- input_grad: float32 [8192, 2048], P(('fsdp', 'tp'))
- attn_gain_grad: float32 [2048], P('fsdp')
- query_grad: float32 [2048, 2048], P('fsdp', 'tp')
- key_grad: float32 [2048, 512], P('fsdp', 'tp')
- value_grad: float32 [2048, 512], P('fsdp', 'tp')
- out_grad: float32 [2048, 2048], P('tp', 'fsdp')
- mlp_gain_grad: float32 [2048], P('fsdp')
- gate_grad: float32 [2048, 8192], P('fsdp', 'tp')
- up_grad: float32 [2048, 8192], P('fsdp', 'tp')
- down_grad: float32 [8192, 2048], P('tp', 'fsdp')
Inputs may be any that keep to these rules, and one draw needn't show every extreme that they name: `segment_ids`: in each tree the trunk, segment 0, fills the first 256 rows; segments 1 to 4 are branches and the rest leaves, each filling one aligned run of 64 rows, in any order. `path_positions`: trunk rows count from 0; a branch's rows from 256, a leaf's from (5) * 64. `ancestor_masks`: the trunk is the parent of every branch, each branch the parent of two leaves; a segment counts as its own ancestor.
All inputs are finite; a program needn't handle non-finite values.
Results may differ from a plain program's by a relative error of at most 0.019.
Values may be sent and summed in bfloat16 or wider, within the bound.
A program may use at most 320 MiB of HBM per device.

v0:
```python
import math
import jax
import jax.numpy as jnp
import numpy as np
from jax import lax
from jax.sharding import PartitionSpec as P

HD = 64
SEGS = 13
EPSILON = 1e-05


def inverse_freq(head_size):
    base_freq = 1.0 / 500000.0 ** (np.arange(0, head_size, 2) / head_size)
    wavelen = 2.0 * math.pi / base_freq
    smooth = (8192.0 / wavelen - 1.0) / 3.0
    blended = (1.0 - smooth) * base_freq / 32.0 + smooth * base_freq
    scaled = np.where(
        wavelen > 8192.0, base_freq / 32.0, np.where(wavelen < 2048.0, base_freq, blended)
    )
    return scaled.astype(np.float32)


def rope_tables(positions, head_size):
    freqs = jnp.asarray(inverse_freq(head_size))
    angles = positions.astype(jnp.float32)[:, None] * freqs[None, :]
    angles = jnp.concatenate([angles, angles], axis=-1)
    return (jnp.cos(angles), jnp.sin(angles))


def rotate_half(values):
    half_size = values.shape[-1] // 2
    return jnp.concatenate([-values[..., half_size:], values[..., :half_size]], axis=-1)


def apply_rope(values, cosine_table, sine_table):
    return values * cosine_table[:, None, :] + rotate_half(values) * sine_table[:, None, :]


def rope_back(gradient, cosine_table, sine_table):
    return gradient * cosine_table[:, None, :] - rotate_half(gradient * sine_table[:, None, :])


def rms_scale(row_values):
    return lax.rsqrt(jnp.mean(row_values * row_values, axis=-1, keepdims=True) + EPSILON)


def norm_back(row_values, row_scale, gain_values, grad_out):
    scaled_grad = grad_out * gain_values
    gain_part = jnp.sum(grad_out * row_values * row_scale, axis=0)
    rows_grad = row_scale * scaled_grad - row_values * row_scale**3 * jnp.mean(
        scaled_grad * row_values, axis=-1, keepdims=True
    )
    return (rows_grad, gain_part)


def contract_rows(left, right):
    return lax.dot_general(
        left, right, (((0,), (0,)), ((), ())), preferred_element_type=jnp.float32
    )


def times_transposed(left, right):
    return lax.dot_general(
        left, right, (((1,), (1,)), ((), ())), preferred_element_type=jnp.float32
    )


def gather_rows(pieces):
    return lax.all_gather(pieces, "tp", axis=0, tiled=True)


def scatter_rows(partial_sums):
    return lax.psum_scatter(partial_sums, "tp", scatter_dimension=0, tiled=True)


def body(
    layer_input,
    cotangent,
    segment_ids,
    path_positions,
    ancestor_masks,
    attn_gain,
    query_weight,
    key_weight,
    value_weight,
    out_weight,
    mlp_gain,
    gate_weight,
    up_weight,
    down_weight,
):
    tree_len = segment_ids.shape[0]
    local_heads = query_weight.shape[1] // HD
    local_groups = key_weight.shape[1] // HD
    group_size = local_heads // local_groups
    score_scale = HD ** (-0.5)
    block_rows = min(512, tree_len)
    cosine_table, sine_table = rope_tables(path_positions, HD)
    segment_hot = (segment_ids[:, None] == jnp.arange(SEGS)[None, :]).astype(jnp.float32)
    ancestor_table = ancestor_masks[0].astype(jnp.float32)
    token_index = jnp.arange(tree_len)

    def allowed_block(row_start):
        hot_rows = segment_hot[row_start : row_start + block_rows]
        reach_rows = jnp.dot(hot_rows, ancestor_table, precision=lax.Precision.HIGHEST)
        reach = times_transposed(reach_rows, segment_hot)
        same_segment = times_transposed(hot_rows, segment_hot)
        causal = token_index[None, :] <= (row_start + jnp.arange(block_rows))[:, None]
        return (reach > 0.5) & ((same_segment < 0.5) | causal)

    query_full, key_full, value_full, gain_first = (
        lax.all_gather(query_weight, "fsdp", axis=0, tiled=True),
        lax.all_gather(key_weight, "fsdp", axis=0, tiled=True),
        lax.all_gather(value_weight, "fsdp", axis=0, tiled=True),
        lax.all_gather(attn_gain, "fsdp", axis=0, tiled=True),
    )
    input_rows = layer_input.astype(jnp.float32)
    first_scale = rms_scale(input_rows)
    first_gain = gain_first.astype(jnp.float32)
    first_normed = gather_rows((input_rows * first_scale * first_gain).astype(jnp.bfloat16))
    query_pre = jnp.dot(first_normed, query_full, preferred_element_type=jnp.float32)
    queries = apply_rope(
        query_pre.reshape(tree_len, local_heads, HD), cosine_table, sine_table
    ).astype(jnp.bfloat16)
    key_pre = jnp.dot(first_normed, key_full, preferred_element_type=jnp.float32)
    key_rows = apply_rope(
        key_pre.reshape(tree_len, local_groups, HD), cosine_table, sine_table
    ).astype(jnp.bfloat16)
    value_rows = (
        jnp.dot(first_normed, value_full, preferred_element_type=jnp.float32)
        .astype(jnp.bfloat16)
        .reshape(tree_len, local_groups, HD)
    )
    query_groups = queries.reshape(tree_len, local_groups, group_size, HD)
    attended_blocks = []
    lse_blocks = []
    for row_start in range(0, tree_len, block_rows):
        allowed = allowed_block(row_start)
        query_block = query_groups[row_start : row_start + block_rows]
        raw_scores = (
            jnp.einsum("qkgd,skd->kgqs", query_block, key_rows, preferred_element_type=jnp.float32)
            * score_scale
        )
        masked = jnp.where(allowed[None, None], raw_scores, -1e30)
        row_max = jnp.max(masked, axis=-1, keepdims=True)
        exponent = jnp.exp(masked - row_max)
        row_total = jnp.sum(exponent, axis=-1, keepdims=True)
        probs_low = (exponent / row_total).astype(jnp.bfloat16)
        mixture = jnp.einsum(
            "kgqs,skd->qkgd", probs_low, value_rows, preferred_element_type=jnp.float32
        )
        attended_blocks.append(mixture.astype(jnp.bfloat16).reshape(block_rows, local_heads * HD))
        lse_blocks.append(row_max + jnp.log(row_total))
    attended = jnp.concatenate(attended_blocks, axis=0)
    out_full = lax.all_gather(out_weight, "fsdp", axis=1, tiled=True)
    residual = input_rows + scatter_rows(
        jnp.dot(attended, out_full, preferred_element_type=jnp.float32)
    )
    gate_full, up_full, gain_second = (
        lax.all_gather(gate_weight, "fsdp", axis=0, tiled=True),
        lax.all_gather(up_weight, "fsdp", axis=0, tiled=True),
        lax.all_gather(mlp_gain, "fsdp", axis=0, tiled=True),
    )
    down_full = lax.all_gather(down_weight, "fsdp", axis=1, tiled=True)
    second_scale = rms_scale(residual)
    second_gain = gain_second.astype(jnp.float32)
    second_normed = gather_rows((residual * second_scale * second_gain).astype(jnp.bfloat16))
    gate_proj = jnp.dot(second_normed, gate_full, preferred_element_type=jnp.float32)
    up_proj = jnp.dot(second_normed, up_full, preferred_element_type=jnp.float32)
    sigmoid_gate = jax.nn.sigmoid(gate_proj)
    hidden = (gate_proj * sigmoid_gate * up_proj).astype(jnp.bfloat16)
    output_rows = residual + scatter_rows(
        jnp.dot(hidden, down_full, preferred_element_type=jnp.float32)
    )
    output = output_rows.astype(jnp.bfloat16)
    gate_used, up_used, down_used = (gate_full, up_full, down_full)
    cot_rows = cotangent.astype(jnp.float32)
    mlp_back = gather_rows(cotangent)
    hidden_back = times_transposed(mlp_back, down_used)
    down_grad = contract_rows(hidden, mlp_back)
    gate_back = (
        hidden_back * up_proj * sigmoid_gate * (1.0 + gate_proj * (1.0 - sigmoid_gate))
    ).astype(jnp.bfloat16)
    up_back = (hidden_back * gate_proj * sigmoid_gate).astype(jnp.bfloat16)
    gate_grad = contract_rows(second_normed, gate_back)
    up_grad = contract_rows(second_normed, up_back)
    second_back = scatter_rows(
        times_transposed(gate_back, gate_used) + times_transposed(up_back, up_used)
    )
    residual_back, mlp_gain_part = norm_back(residual, second_scale, second_gain, second_back)
    residual_back = residual_back + cot_rows
    branch_back = gather_rows(residual_back.astype(jnp.bfloat16))
    attended_back = times_transposed(branch_back, out_full).astype(jnp.bfloat16)
    out_grad = contract_rows(attended, branch_back)
    key_accum = jnp.zeros((tree_len, local_groups, HD), jnp.float32)
    value_accum = jnp.zeros((tree_len, local_groups, HD), jnp.float32)
    query_blocks = []
    for block_index, row_start in enumerate(range(0, tree_len, block_rows)):
        allowed = allowed_block(row_start)
        query_block = query_groups[row_start : row_start + block_rows]
        raw_scores = (
            jnp.einsum("qkgd,skd->kgqs", query_block, key_rows, preferred_element_type=jnp.float32)
            * score_scale
        )
        masked = jnp.where(allowed[None, None], raw_scores, -1e30)
        prob_block = jnp.exp(masked - lse_blocks[block_index])
        probs_low = prob_block.astype(jnp.bfloat16)
        grad_block = attended_back[row_start : row_start + block_rows].reshape(
            block_rows, local_groups, group_size, HD
        )
        prob_back = jnp.einsum(
            "qkgd,skd->kgqs", grad_block, value_rows, preferred_element_type=jnp.float32
        )
        row_delta = jnp.sum(prob_block * prob_back, axis=-1, keepdims=True)
        score_back = (prob_block * (prob_back - row_delta)).astype(jnp.bfloat16)
        query_blocks.append(
            jnp.einsum("kgqs,skd->qkgd", score_back, key_rows, preferred_element_type=jnp.float32)
            * score_scale
        )
        key_accum = (
            key_accum
            + jnp.einsum(
                "kgqs,qkgd->skd", score_back, query_block, preferred_element_type=jnp.float32
            )
            * score_scale
        )
        value_accum = value_accum + jnp.einsum(
            "kgqs,qkgd->skd", probs_low, grad_block, preferred_element_type=jnp.float32
        )
    query_accum = jnp.concatenate(query_blocks, axis=0).reshape(tree_len, local_heads, HD)
    query_back = (
        rope_back(query_accum, cosine_table, sine_table)
        .astype(jnp.bfloat16)
        .reshape(tree_len, local_heads * HD)
    )
    key_back = (
        rope_back(key_accum, cosine_table, sine_table)
        .astype(jnp.bfloat16)
        .reshape(tree_len, local_groups * HD)
    )
    value_back = value_accum.astype(jnp.bfloat16).reshape(tree_len, local_groups * HD)
    query_grad = contract_rows(first_normed, query_back)
    key_grad = contract_rows(first_normed, key_back)
    value_grad = contract_rows(first_normed, value_back)
    first_back = scatter_rows(
        times_transposed(query_back, query_full)
        + times_transposed(key_back, key_full)
        + times_transposed(value_back, value_full)
    )
    input_grad, attn_gain_part = norm_back(input_rows, first_scale, first_gain, first_back)
    input_grad = input_grad + residual_back
    attn_gain_sum, query_sum, key_sum, value_sum, mlp_gain_sum, gate_sum, up_sum = (
        lax.psum_scatter(
            attn_gain_part.astype(jnp.bfloat16), "fsdp", scatter_dimension=0, tiled=True
        ).astype(jnp.float32),
        lax.psum_scatter(
            query_grad.astype(jnp.bfloat16), "fsdp", scatter_dimension=0, tiled=True
        ).astype(jnp.float32),
        lax.psum_scatter(
            key_grad.astype(jnp.bfloat16), "fsdp", scatter_dimension=0, tiled=True
        ).astype(jnp.float32),
        lax.psum_scatter(
            value_grad.astype(jnp.bfloat16), "fsdp", scatter_dimension=0, tiled=True
        ).astype(jnp.float32),
        lax.psum_scatter(
            mlp_gain_part.astype(jnp.bfloat16), "fsdp", scatter_dimension=0, tiled=True
        ).astype(jnp.float32),
        lax.psum_scatter(
            gate_grad.astype(jnp.bfloat16), "fsdp", scatter_dimension=0, tiled=True
        ).astype(jnp.float32),
        lax.psum_scatter(
            up_grad.astype(jnp.bfloat16), "fsdp", scatter_dimension=0, tiled=True
        ).astype(jnp.float32),
    )
    out_sum, down_sum = (
        lax.psum_scatter(
            out_grad.astype(jnp.bfloat16), "fsdp", scatter_dimension=1, tiled=True
        ).astype(jnp.float32),
        lax.psum_scatter(
            down_grad.astype(jnp.bfloat16), "fsdp", scatter_dimension=1, tiled=True
        ).astype(jnp.float32),
    )
    attn_gain_total, mlp_gain_total = lax.psum((attn_gain_sum, mlp_gain_sum), "tp")
    return (
        output,
        input_grad,
        attn_gain_total,
        query_sum,
        key_sum,
        value_sum,
        out_sum,
        mlp_gain_total,
        gate_sum,
        up_sum,
        down_sum,
    )


def solution(mesh):
    return jax.shard_map(
        body,
        mesh=mesh,
        in_specs=(
            P(("fsdp", "tp"), None),
            P(("fsdp", "tp"), None),
            P("fsdp"),
            P("fsdp"),
            P("fsdp", None, None),
            P("fsdp"),
            P("fsdp", "tp"),
            P("fsdp", "tp"),
            P("fsdp", "tp"),
            P("tp", "fsdp"),
            P("fsdp"),
            P("fsdp", "tp"),
            P("fsdp", "tp"),
            P("tp", "fsdp"),
        ),
        out_specs=(
            P(("fsdp", "tp"), None),
            P(("fsdp", "tp"), None),
            P("fsdp"),
            P("fsdp", "tp"),
            P("fsdp", "tp"),
            P("fsdp", "tp"),
            P("tp", "fsdp"),
            P("fsdp"),
            P("fsdp", "tp"),
            P("fsdp", "tp"),
            P("tp", "fsdp"),
        ),
        check_vma=False,
    )
```

profile of v0, /device:TPU:0, one launch (start us, length us, event | category | flops | bytes accessed | tf_op | source)
XLA Modules:
  0.0 1434.2 jit_solution(2800710086688930849)
XLA Ops:
  10.0 13.4 all-gather
  31.4 15.0 %all_gather.42 = bf16[2048,128]{1,0:T(8,128)(2,1)S(1)} all-gather(bf16[256,128]{1,0:T(8,128)(2,1)S(1)} %copy-done.37), channel_id=1, replica_groups=mesh['fsdp'=8,'tp'=4] {'fsdp'}, dimensions={0}, use_global_device_ids=true | all-gather | bytes 589824 | tf_op jit(solution)/shard_map/all_gather | solution.py:114
  46.4 15.0 %all_gather.41 = bf16[2048,128]{1,0:T(8,128)(2,1)S(1)} all-gather(bf16[256,128]{1,0:T(8,128)(2,1)S(1)} %copy-done.38), channel_id=1, replica_groups=mesh['fsdp'=8,'tp'=4] {'fsdp'}, dimensions={0}, use_global_device_ids=true | all-gather | bytes 589824 | tf_op jit(solution)/shard_map/all_gather | solution.py:115
  68.4 9.3 all-gather.12.cloned.1.call-done
  81.5 27.0 %all-gather.14.cloned.1.call-done = bf16[2048,512]{1,0:T(8,128)(2,1)} async-done(((bf16[256,512]{1,0:T(8,128)(2,1)}), bf16[2048,512]{1,0:T(8,128)(2,1)}) %all-gather.14.cloned.1.call-update) | async-done | bytes 2097168 | tf_op jit(solution)/shard_map/all_gather | solution.py:113
  108.4 5.2 fusion.83
  116.6 7.3 fusion.80
  123.9 8.3 fusion.7
  133.8 8.1 fusion.36
  142.0 7.3 fusion.81
  149.2 8.1 fusion.6
  157.9 7.4 fusion.37
  165.4 7.5 fusion.52
  173.5 10.3 all-gather.1
  183.9 75.0 %reduce-scatter.12.cloned.1.call-done = f32[256,2048]{1,0:T(8,128)} async-done(((f32[1024,2048]{1,0:T(8,128)}), f32[256,2048]{1,0:T(8,128)}) %reduce-scatter.12.cloned.1.call-update) | async-done | bytes 2097168 | tf_op jit(solution)/shard_map/reduce_scatter | solution.py:74
  264.4 78.1 %all-gather.22.cloned.1.call-done = bf16[2048,2048]{1,0:T(8,128)(2,1)} async-done(((bf16[256,2048]{1,0:T(8,128)(2,1)}), bf16[2048,2048]{1,0:T(8,128)(2,1)}) %all-gather.22.cloned.1.call-update) | async-done | bytes 8388624 | tf_op jit(solution)/shard_map/all_gather | solution.py:162
  342.5 53.7 %all-gather.18.cloned.1.call-done = bf16[1024,2048]{1,0:T(8,128)(2,1)} async-done(((bf16[256,2048]{1,0:T(8,128)(2,1)}), bf16[1024,2048]{1,0:T(8,128)(2,1)}) %all-gather.18.cloned.1.call-update) | async-done | bytes 4194320 | tf_op jit(solution)/shard_map/all_gather | solution.py:70
  396.2 14.7 %fusion.85 = f32[1024,2048]{1,0:T(8,128)} fusion(bf16[1024,2048]{1,0:T(8,128)(2,1)} %all-gather.18.cloned.1.call-done, bf16[2048,2048]{1,0:T(8,128)(2,1)} %all-gather.22.cloned.1.call-done), kind=kOutput, calls=%fused_computation.150 | convolution fusion | flops 8589934592 | bytes 20971520 | tf_op jit(solution)/shard_map/dot_general | solution.py:170
  410.9 69.1 %all-gather.20.cloned.1.call-done = bf16[2048,2048]{1,0:T(8,128)(2,1)} async-done(((bf16[256,2048]{1,0:T(8,128)(2,1)}), bf16[2048,2048]{1,0:T(8,128)(2,1)}) %all-gather.20.cloned.1.call-update) | async-done | bytes 8388624 | tf_op jit(solution)/shard_map/all_gather | solution.py:161
  480.0 14.4 %fusion.84 = f32[1024,2048]{1,0:T(8,128)} fusion(bf16[1024,2048]{1,0:T(8,128)(2,1)} %all-gather.18.cloned.1.call-done, bf16[2048,2048]{1,0:T(8,128)(2,1)} %all-gather.20.cloned.1.call-done), kind=kOutput, calls=%fused_computation.149 | convolution fusion | flops 8589934592 | bytes 20971520 | tf_op jit(solution)/shard_map/dot_general | solution.py:169
  494.4 38.8 %all-gather.26.cloned.1.call-done = bf16[1024,2048]{1,0:T(8,128)(2,1)} async-done(((bf16[256,2048]{1,0:T(8,128)(2,1)}), bf16[1024,2048]{1,0:T(8,128)(2,1)}) %all-gather.26.cloned.1.call-update) | async-done | bytes 4194320 | tf_op jit(solution)/shard_map/all_gather | solution.py:70
  533.2 84.2 %all-gather.24.cloned.1.call-done = bf16[2048,2048]{1,0:T(8,128)(2,1)} async-done(((bf16[2048,256]{1,0:T(8,128)(2,1)}), bf16[2048,2048]{1,0:T(8,128)(2,1)}) %all-gather.24.cloned.1.call-update) | async-done | bytes 8388624 | tf_op jit(solution)/shard_map/all_gather | solution.py:165
  617.5 21.8 %multiply_convert_fusion = (bf16[1024,2048]{1,0:T(8,128)(2,1)}, bf16[1024,2048]{1,0:T(8,128)(2,1)}, bf16[1024,2048]{1,0:T(8,128)(2,1)}) fusion(f32[1024,2048]{1,0:T(8,128)} %fusion.84, f32[1024,2048]{1,0:T(8,128)} %fusion.85, bf16[1024,2048]{1,0:T(8,128)(2,1)} %all-gather.26.cloned.1.call-done, bf16[2048,2048]{1,0:T(8,128)(2,1)} %all-gather.24.cloned.1.call-done), kind=kOutput, calls=%fused_computation.26 | convolution fusion | flops 8623489024 | bytes 41943040 | tf_op jit(solution)/shard_map/dot_general | solution.py:64
  639.3 12.9 fusion.87
  652.2 13.5 convolution_add_fusion
  665.8 14.5 %fusion.86 = f32[1024,2048]{1,0:T(8,128)} fusion(bf16[1024,2048]{1,0:T(8,128)(2,1)} %get-tuple-element.25, bf16[2048,2048]{1,0:T(8,128)(2,1)} %all-gather.24.cloned.1.call-done), kind=kOutput, calls=%fused_computation.151 | convolution fusion | flops 8589934592 | bytes 20971520 | tf_op jit(solution)/shard_map/dot_general | solution.py:174
  680.4 70.1 %reduce-scatter.16.cloned.1.call-done = f32[256,2048]{1,0:T(8,128)} async-done(((f32[1024,2048]{1,0:T(8,128)}), f32[256,2048]{1,0:T(8,128)}) %reduce-scatter.16.cloned.1.call-update) | async-done | bytes 2097168 | tf_op jit(solution)/shard_map/reduce_scatter | solution.py:74
  753.2 86.8 %reduce-scatter.14.cloned.1.call-done = f32[256,2048]{1,0:T(8,128)} async-done(((f32[1024,2048]{1,0:T(8,128)}), f32[256,2048]{1,0:T(8,128)}) %reduce-scatter.14.cloned.1.call-update) | async-done | bytes 2097168 | tf_op jit(solution)/shard_map/reduce_scatter | solution.py:74
  845.1 14.5 %convolution_convert_fusion = bf16[2048,2048]{1,0:T(8,128)(2,1)} fusion(bf16[1024,2048]{1,0:T(8,128)(2,1)} %get-tuple-element.25, bf16[1024,2048]{1,0:T(8,128)(2,1)} %all-gather.26.cloned.1.call-done), kind=kOutput, calls=%fused_computation.33 | convolution fusion | flops 8594128896 | bytes 16777216 | tf_op jit(solution)/shard_map/dot_general | solution.py:58
  859.6 14.1 convolution_convert_fusion.1
  873.8 14.3 convolution_convert_fusion.2
  888.9 9.0 all-gather.28.cloned.1.call-done
  903.5 10.8 fusion.38
  922.4 15.1 %fusion = (f32[2,4,512]{2,1,0:T(4,128)S(1)}, f32[2,1024,512,4]{2,1,3,0:T(8,128)}) fusion(f32[2,4,512,1024]{2,3,1,0:T(8,128)} %get-tuple-element.48, f32[2,4,512]{2,1,0:T(4,128)S(1)} %bitcast.189, bf16[1024,2,64,1]{0,2,3,1:T(8,128)(2,1)} %bitcast.179, bf16[512,2,4,64]{0,3,2,1:T(8,128)(2,1)} %bitcast.170), kind=kOutput, calls=%fused_computation.2 | convolution fusion | flops 549449728 | bytes 34373632 | tf_op jit(solution)/shard_map/qkgd,skd->kgqs/dot_general | solution.py:212
  937.6 12.3 fusion.2
  955.9 7.6 fusion.3
  963.5 12.4 fusion.5
  983.5 6.0 convolution_convert_fusion.3
  994.5 5.7 fusion.35
  1021.6 58.6 %reduce-scatter.30.cloned.1.call-done = bf16[256,2048]{1,0:T(8,128)(2,1)} async-done(((bf16[2048,2048]{1,0:T(8,128)(2,1)}), bf16[256,2048]{1,0:T(8,128)(2,1)}) %reduce-scatter.30.cloned.1.call-update) | async-done | bytes 1048592 | tf_op jit(solution)/shard_map/reduce_scatter | solution.py:272
  1083.0 87.4 %reduce-scatter.28.cloned.1.call-done = bf16[256,2048]{1,0:T(8,128)(2,1)} async-done(((bf16[2048,2048]{1,0:T(8,128)(2,1)}), bf16[256,2048]{1,0:T(8,128)(2,1)}) %reduce-scatter.28.cloned.1.call-update) | async-done | bytes 1048592 | tf_op jit(solution)/shard_map/reduce_scatter | solution.py:269
  1173.2 28.7 %reduce-scatter.24.cloned.1.call-done = bf16[256,128]{1,0:T(8,128)(2,1)} async-done(((bf16[2048,128]{1,0:T(8,128)(2,1)}), bf16[256,128]{1,0:T(8,128)(2,1)}) %reduce-scatter.24.cloned.1.call-update) | async-done | bytes 65552 | tf_op jit(solution)/shard_map/reduce_scatter | solution.py:263
  1203.4 30.3 %reduce-scatter.22.cloned.1.call-done = bf16[256,128]{1,0:T(8,128)(2,1)} async-done(((bf16[2048,128]{1,0:T(8,128)(2,1)}), bf16[256,128]{1,0:T(8,128)(2,1)}) %reduce-scatter.22.cloned.1.call-update) | async-done | bytes 65552 | tf_op jit(solution)/shard_map/reduce_scatter | solution.py:260
  1235.3 34.8 %reduce-scatter.26.cloned.1.call-done = bf16[512,256]{1,0:T(8,128)(2,1)} async-done(((bf16[512,2048]{1,0:T(8,128)(2,1)}), bf16[512,256]{1,0:T(8,128)(2,1)}) %reduce-scatter.26.cloned.1.call-update) | async-done | bytes 262160 | tf_op jit(solution)/shard_map/reduce_scatter | solution.py:277
  1271.9 35.1 %reduce-scatter.20.cloned.1.call-done = bf16[256,512]{1,0:T(8,128)(2,1)} async-done(((bf16[2048,512]{1,0:T(8,128)(2,1)}), bf16[256,512]{1,0:T(8,128)(2,1)}) %reduce-scatter.20.cloned.1.call-update) | async-done | bytes 262160 | tf_op jit(solution)/shard_map/reduce_scatter | solution.py:257
  1308.8 86.5 %reduce-scatter.18.cloned.1.call-done = f32[256,2048]{1,0:T(8,128)} async-done(((f32[1024,2048]{1,0:T(8,128)}), f32[256,2048]{1,0:T(8,128)}) %reduce-scatter.18.cloned.1.call-update) | async-done | bytes 2097168 | tf_op jit(solution)/shard_map/reduce_scatter | solution.py:74
  1397.6 16.6 %all-reduce.3 = (bf16[2048]{0:T(1024)(128)(2,1)S(1)}, bf16[2048]{0:T(1024)(128)(2,1)S(1)}) all-reduce(bf16[2048]{0:T(1024)(128)(2,1)S(1)} %get-tuple-element.13, bf16[2048]{0:T(1024)(128)(2,1)S(1)} %copy-done.46), channel_id=6, replica_groups=mesh['fsdp'=8,'tp'=4] {'fsdp'}, use_global_device_ids=true, to_apply=%region_15.16.clone | all-reduce | flops 4096 | bytes 16384
  1414.2 9.4 all-reduce.2
  (247 shorter events, 111.9 us)
Async XLA Ops:
  7.2 21.0 %copy-start.47 = (s32[1,13,13]{2,0,1:T(1,128)S(1)}, s32[1,13,13]{2,0,1:T(1,128)}, u32[]{:S(2)}) copy-start(s32[1,13,13]{2,0,1:T(1,128)} %param.19) | copy-start | bytes 2032
  7.2 21.0 %copy-start.43 = (s32[1024]{0:T(1024)S(1)}, s32[1024]{0:T(1024)}, u32[]{:S(2)}) copy-start(s32[1024]{0:T(1024)} %param.17) | copy-start | bytes 12292
  7.2 70.5 %all-gather.12.cloned.1.call-start = ((), (), s32[]{:S(2)}) async-start(), calls=%async_computation.11 | async-start | bytes 5242880 | tf_op jit(solution)/shard_map/all_gather | solution.py:70
  10.0 21.4 %copy-start.44 = (f32[256]{0:T(256)}, f32[256]{0:T(256)S(1)}, u32[]{:S(2)}) copy-start(f32[256]{0:T(256)S(1)} %get-tuple-element.44) | copy-start | bytes 3076
  24.1 22.3 %copy-start.38 = (bf16[256,128]{1,0:T(8,128)(2,1)S(1)}, bf16[256,128]{1,0:T(8,128)(2,1)}, u32[]{:S(2)}) copy-start(bf16[256,128]{1,0:T(8,128)(2,1)} %param.23) | copy-start | bytes 196612
  26.6 34.7 %copy-start.50 = (f32[32]{0:T(128)S(1)}, f32[32]{0:T(128)}, u32[]{:S(2)}) copy-start(f32[32]{0:T(128)} %constant.26.clone) | copy-start | bytes 388
  26.6 81.8 %all-gather.14.cloned.1.call-start = ((), (), s32[]{:S(2)}) async-start(), calls=%async_computation.12 | async-start | bytes 2359296 | tf_op jit(solution)/shard_map/all_gather | solution.py:113
  27.4 138.0 %all-gather.16.cloned.1.call-start = ((), (), s32[]{:S(2)}) async-start(), calls=%async_computation.13 | async-start | bytes 2359296 | tf_op jit(solution)/shard_map/all_gather | solution.py:156
  28.1 230.8 %reduce-scatter.12.cloned.1.call-start = ((), (), s32[]{:S(2)}) async-start(), calls=%async_computation.14 | async-start | bytes 10485760 | tf_op jit(solution)/shard_map/reduce_scatter | solution.py:74
  46.4 31.4 %copy-start.15 = (bf16[2048,128]{1,0:T(8,128)(2,1)}, bf16[2048,128]{1,0:T(8,128)(2,1)S(1)}, u32[]{:S(2)}) copy-start(bf16[2048,128]{1,0:T(8,128)(2,1)S(1)} %all_gather.42) | copy-start | bytes 1572868
  61.3 70.9 %copy-start.13 = (bf16[2048,128]{1,0:T(8,128)(2,1)}, bf16[2048,128]{1,0:T(8,128)(2,1)S(1)}, u32[]{:S(2)}) copy-start(bf16[2048,128]{1,0:T(8,128)(2,1)S(1)} %all_gather.41) | copy-start | bytes 1572868
  63.4 50.4 %copy-start.24 = (f32[1024,64]{0,1:T(8,128)}, f32[1024,64]{0,1:T(8,128)S(1)}, u32[]{:S(2)}) copy-start(f32[1024,64]{0,1:T(8,128)S(1)} %get-tuple-element.42) | copy-start | bytes 786436
  63.4 51.9 %copy-start.22 = (f32[1024,64]{0,1:T(8,128)}, f32[1024,64]{0,1:T(8,128)S(1)}, u32[]{:S(2)}) copy-start(f32[1024,64]{0,1:T(8,128)S(1)} %get-tuple-element.41) | copy-start | bytes 786436
  116.6 25.4 %copy-start.9 = (bf16[1024,2,64,1]{0,2,3,1:T(8,128)(2,1)}, bf16[1024,2,64,1]{0,2,3,1:T(8,128)(2,1)S(1)}, u32[]{:S(2)}) copy-start(bf16[1024,2,64,1]{0,2,3,1:T(8,128)(2,1)S(1)} %fusion.58) | copy-start | bytes 786436
  133.8 23.5 %copy-start.26 = (bf16[1024,128]{0,1:T(8,128)(2,1)}, bf16[1024,128]{0,1:T(8,128)(2,1)S(1)}, u32[]{:S(2)}) copy-start(bf16[1024,128]{0,1:T(8,128)(2,1)S(1)} %convolution_convert_fusion.8) | copy-start | bytes 786436
  141.9 23.4 %copy-start.54 = (bf16[2,64,4,512]{3,1,2,0:T(8,128)(2,1)}, bf16[2,64,4,512]{3,1,2,0:T(8,128)(2,1)S(1)}, u32[]{:S(2)}) copy-start(bf16[2,64,4,512]{3,1,2,0:T(8,128)(2,1)S(1)} %fusion.36) | copy-start | bytes 1572868
  172.8 86.1 %copy-start.2 = (bf16[256,2048]{1,0:T(8,128)(2,1)S(1)}, bf16[256,2048]{1,0:T(8,128)(2,1)}, u32[]{:S(2)}) copy-start(bf16[256,2048]{1,0:T(8,128)(2,1)} %param.15) | copy-start | bytes 3145732
  172.9 169.7 %all-gather.22.cloned.1.call-start = ((), (), s32[]{:S(2)}) async-start(), calls=%async_computation.17 | async-start | bytes 9437184 | tf_op jit(solution)/shard_map/all_gather | solution.py:162
  173.4 222.8 %all-gather.18.cloned.1.call-start = ((), (), s32[]{:S(2)}) async-start(), calls=%async_computation.15 | async-start | bytes 5242880 | tf_op jit(solution)/shard_map/all_gather | solution.py:70
  262.1 217.9 %all-gather.20.cloned.1.call-start = ((), (), s32[]{:S(2)}) async-start(), calls=%async_computation.16 | async-start | bytes 9437184 | tf_op jit(solution)/shard_map/all_gather | solution.py:161
  262.9 270.4 %all-gather.26.cloned.1.call-start = ((), (), s32[]{:S(2)}) async-start(), calls=%async_computation.20 | async-start | bytes 5242880 | tf_op jit(solution)/shard_map/all_gather | solution.py:70
  263.6 353.9 %all-gather.24.cloned.1.call-start = ((), (), s32[]{:S(2)}) async-start(), calls=%async_computation.18 | async-start | bytes 9437184 | tf_op jit(solution)/shard_map/all_gather | solution.py:165
  264.3 486.2 %reduce-scatter.16.cloned.1.call-start = ((), (), s32[]{:S(2)}) async-start(), calls=%async_computation.21 | async-start | bytes 10485760 | tf_op jit(solution)/shard_map/reduce_scatter | solution.py:74
  639.3 12.9 copy-start.59
  665.8 174.3 %reduce-scatter.14.cloned.1.call-start = ((), (), s32[]{:S(2)}) async-start(), calls=%async_computation.19 | async-start | bytes 10485760 | tf_op jit(solution)/shard_map/reduce_scatter | solution.py:74
  680.3 159.7 %copy-start.21 = (bf16[256,2048]{1,0:T(8,128)(2,1)S(1)}, bf16[256,2048]{1,0:T(8,128)(2,1)}, u32[]{:S(2)}) copy-start(bf16[256,2048]{1,0:T(8,128)(2,1)} %param.16) | copy-start | bytes 3145732
  680.3 217.6 %all-gather.28.cloned.1.call-start = ((), (), s32[]{:S(2)}) async-start(), calls=%async_computation.22 | async-start | bytes 5242880 | tf_op jit(solution)/shard_map/all_gather | solution.py:70
  845.0 173.8 %reduce-scatter.32.cloned.1.call-start = ((), (), s32[]{:S(2)}) async-start(), calls=%async_computation.30 | async-start | bytes 9437184 | tf_op jit(solution)/shard_map/reduce_scatter | solution.py:280
  859.6 220.6 %reduce-scatter.30.cloned.1.call-start = ((), (), s32[]{:S(2)}) async-start(), calls=%async_computation.29 | async-start | bytes 9437184 | tf_op jit(solution)/shard_map/reduce_scatter | solution.py:272
  873.8 296.6 %reduce-scatter.28.cloned.1.call-start = ((), (), s32[]{:S(2)}) async-start(), calls=%async_computation.28 | async-start | bytes 9437184 | tf_op jit(solution)/shard_map/reduce_scatter | solution.py:269
  888.1 313.8 %reduce-scatter.24.cloned.1.call-start = ((), (), s32[]{:S(2)}) async-start(), calls=%async_computation.26 | async-start | bytes 589824 | tf_op jit(solution)/shard_map/reduce_scatter | solution.py:263
  897.9 16.4 %slice-start.4 = ((s8[16777216]{0:T(1024)(128)(4,1)}), s8[4194304]{0:T(1024)(128)(4,1)S(1)}, s32[]{:S(2)}) async-start(s8[16777216]{0:T(1024)(128)(4,1)} %bitcast.163), calls=%async_computation.35 | async-start | bytes 8388608
  897.9 16.4 %slice-start.5 = ((s8[16777216]{0:T(1024)(128)(4,1)}), s8[4194304]{0:T(1024)(128)(4,1)S(1)}, s32[]{:S(2)}) async-start(s8[16777216]{0:T(1024)(128)(4,1)} %bitcast.163), calls=%async_computation.36 | async-start | bytes 8388608
  922.4 33.4 %slice-start = ((s8[16777216]{0:T(1024)(128)(4,1)}), s8[4194304]{0:T(1024)(128)(4,1)S(1)}, s32[]{:S(2)}) async-start(s8[16777216]{0:T(1024)(128)(4,1)} %bitcast.161), calls=%async_computation.31 | async-start | bytes 8388608
  922.4 33.4 %slice-start.1 = ((s8[16777216]{0:T(1024)(128)(4,1)}), s8[4194304]{0:T(1024)(128)(4,1)S(1)}, s32[]{:S(2)}) async-start(s8[16777216]{0:T(1024)(128)(4,1)} %bitcast.161), calls=%async_computation.32 | async-start | bytes 8388608
  937.5 15.6 %copy-start.18 = (bf16[512,8,64]{0,2,1:T(8,128)(2,1)S(1)}, bf16[512,8,64]{0,2,1:T(8,128)(2,1)}, u32[]{:S(2)}) copy-start(bf16[512,8,64]{0,2,1:T(8,128)(2,1)} %copy-done.17) | copy-start | bytes 1572868
  937.5 18.3 %slice-start.2 = ((s8[16777216]{0:T(1024)(128)(4,1)}), s8[4194304]{0:T(1024)(128)(4,1)S(1)}, s32[]{:S(2)}) async-start(s8[16777216]{0:T(1024)(128)(4,1)} %bitcast.161), calls=%async_computation.33 | async-start | bytes 8388608
  937.6 18.3 %slice-start.3 = ((s8[16777216]{0:T(1024)(128)(4,1)}), s8[4194304]{0:T(1024)(128)(4,1)S(1)}, s32[]{:S(2)}) async-start(s8[16777216]{0:T(1024)(128)(4,1)} %bitcast.161), calls=%async_computation.34 | async-start | bytes 8388608
  963.5 270.3 %reduce-scatter.22.cloned.1.call-start = ((), (), s32[]{:S(2)}) async-start(), calls=%async_computation.25 | async-start | bytes 589824 | tf_op jit(solution)/shard_map/reduce_scatter | solution.py:260
  983.4 286.7 %reduce-scatter.26.cloned.1.call-start = ((), (), s32[]{:S(2)}) async-start(), calls=%async_computation.27 | async-start | bytes 2359296 | tf_op jit(solution)/shard_map/reduce_scatter | solution.py:277
  989.5 317.5 %reduce-scatter.20.cloned.1.call-start = ((), (), s32[]{:S(2)}) async-start(), calls=%async_computation.24 | async-start | bytes 2359296 | tf_op jit(solution)/shard_map/reduce_scatter | solution.py:257
  1008.0 387.3 %reduce-scatter.18.cloned.1.call-start = ((), (), s32[]{:S(2)}) async-start(), calls=%async_computation.23 | async-start | bytes 10485760 | tf_op jit(solution)/shard_map/reduce_scatter | solution.py:74
  1021.6 373.7 %copy-start.3 = (bf16[256,2048]{1,0:T(8,128)(2,1)S(1)}, bf16[256,2048]{1,0:T(8,128)(2,1)}, u32[]{:S(2)}) copy-start(bf16[256,2048]{1,0:T(8,128)(2,1)} %param.15) | copy-start | bytes 3145732
  1021.6 373.7 %copy-start.36 = (f32[8,1,256]{2,1,0:T(1,128)S(1)}, f32[8,1,256]{2,1,0:T(1,128)}, u32[]{:S(2)}) copy-start(f32[8,1,256]{2,1,0:T(1,128)} %copy-done.35) | copy-start | bytes 24580
  1021.6 373.7 %copy-start.45 = (f32[256]{0:T(256)S(1)}, f32[256]{0:T(256)}, u32[]{:S(2)}) copy-start(f32[256]{0:T(256)} %copy-done.44) | copy-start | bytes 3076
  1083.0 314.6 %copy-start.46 = (bf16[2048]{0:T(1024)(128)(2,1)S(1)}, bf16[2048]{0:T(1024)(128)(2,1)}, u32[]{:S(2)}) copy-start(bf16[2048]{0:T(1024)(128)(2,1)} %get-tuple-element.11) | copy-start | bytes 12292
  1083.0 340.7 %copy-start.48 = (f32[256]{0:T(256)S(1)}, f32[256]{0:T(256)}, u32[]{:S(2)}) copy-start(f32[256]{0:T(256)} %get-tuple-element.43) | copy-start | bytes 3076
  1395.3 28.4 %copy-start.8 = (f32[256,2048]{1,0:T(8,128)S(1)}, f32[256,2048]{1,0:T(8,128)}, u32[]{:S(2)}) copy-start(f32[256,2048]{1,0:T(8,128)} %reduce-scatter.18.cloned.1.call-done) | copy-start | bytes 6291460
  (40 other events, 203.2 us)
Sparse Core Ops, SparseCore 0:
  26.7 50.9 all-gather.11
  79.3 29.0 all-gather.13
  110.0 30.3 all-gather.15
  173.0 85.8 reduce-scatter.11
  260.4 82.0 all-gather.21
  344.9 51.2 all-gather.17
  397.9 82.0 all-gather.19
  482.0 51.2 all-gather.25
  534.9 82.4 all-gather.23
  665.9 84.5 reduce-scatter.15
  753.6 86.3 reduce-scatter.13
  845.2 52.6 all-gather.27
  900.3 89.5 reduce-scatter.31
  992.2 87.9 reduce-scatter.29
  1082.4 87.9 reduce-scatter.27
  1172.6 29.2 reduce-scatter.23
  1204.6 29.1 reduce-scatter.21
  1236.0 34.0 reduce-scatter.25
  1272.5 34.4 reduce-scatter.19
  1310.2 85.0 reduce-scatter.17
where the time goes:
time: 1440 us; the launch traced here: 1430 us
  waiting for transfers between devices  967 us (67%)
  matrix products  271 us (19%)
  other arithmetic  83.3 us (6%)
  blocking collectives  79.7 us (6%)
  between operations  16 us (1%)
  local copies, waits for them, and re-layouts  15.7 us (1%)
    reduce_scatter x4, waiting for transfers between devices, scatter_rows(): return lax.psum_scatter(partial_sums, 'tp', scatter_dimension=0, tiled=True)  318 us
    all_gather x4, waiting for transfers between devices, gather_rows(): return lax.all_gather(pieces, 'tp', axis=0, tiled=True)  111 us
    reduce_scatter x1, waiting for transfers between devices, body(): lax.psum_scatter(gate_grad.astype(jnp.bfloat16), 'fsdp', scatter_dimensio...  87.4 us
    all_gather x1, waiting for transfers between devices, body(): down_full = lax.all_gather(down_weight, 'fsdp', axis=1, tiled=True)  84.2 us
    all_gather x1, waiting for transfers between devices, body(): lax.all_gather(up_weight, 'fsdp', axis=0, tiled=True)  78.1 us
    all_gather x1, waiting for transfers between devices, body(): lax.all_gather(gate_weight, 'fsdp', axis=0, tiled=True)  69.1 us
    dot_general x11, matrix products, times_transposed(): lax.dot_general(left, right, (((1,), (1,)), ((), ())), preferred_element_...  66.9 us
    reduce_scatter x1, waiting for transfers between devices, body(): lax.psum_scatter(up_grad.astype(jnp.bfloat16), 'fsdp', scatter_dimension=...  58.6 us
  transfers between devices with their start and end apart: 20, of which 18 were waited for; matrix products, arithmetic and copies ran while one was open for 20% of the time, Pallas kernels for 0%

commit v1 on v0

--- a/solution.py
+++ b/solution.py
@@ -162,7 +162,12 @@
         lax.all_gather(up_weight, "fsdp", axis=0, tiled=True),
         lax.all_gather(mlp_gain, "fsdp", axis=0, tiled=True),
     )
-    down_full = lax.all_gather(down_weight, "fsdp", axis=1, tiled=True)
+    ring = [down_weight]
+    for hop in range(7):
+        ring.append(lax.ppermute(ring[-1], "fsdp", [(dev, (dev + 1) % 8) for dev in range(8)]))
+    down_full = jnp.roll(
+        jnp.concatenate(ring[::-1], axis=1), (lax.axis_index("fsdp") + 1) * ring[0].shape[1], axis=1
+    )
     second_scale = rms_scale(residual)
     second_gain = gain_second.astype(jnp.float32)
     second_normed = gather_rows((residual * second_scale * second_gain).astype(jnp.bfloat16))

time: 1440 us -> 1390 us (0.965)
  waiting for transfers between devices: 967 us -> 881 us
  local copies, waits for them, and re-layouts: 15.7 us -> 42.2 us
    ppermute x0 -> x7, waiting for transfers between devices: none -> 169 us  [body(): lax.ppermute(ring[-1], 'fsdp', [(dev, (dev + 1) % 8) for dev in range(8)])]
    reduce_scatter x1, waiting for transfers between devices: 0.02 us -> 87.4 us  [body(): lax.psum_scatter(down_grad.astype(jnp.bfloat16), 'fsdp', scatter_dimensio...]
    reduce_scatter x1, waiting for transfers between devices: 87.4 us -> 0.02 us  [body(): lax.psum_scatter(gate_grad.astype(jnp.bfloat16), 'fsdp', scatter_dimensio...]
    all_gather x1 -> x0, waiting for transfers between devices: 84.2 us -> none  [body(): down_full = lax.all_gather(down_weight, 'fsdp', axis=1, tiled=True)]
    all_gather x1, waiting for transfers between devices: 69.1 us -> 0.01 us  [body(): lax.all_gather(gate_weight, 'fsdp', axis=0, tiled=True)]
    all_gather x4, waiting for transfers between devices: 111 us -> 54.3 us  [gather_rows(): return lax.all_gather(pieces, 'tp', axis=0, tiled=True)]
    all_gather x1, waiting for transfers between devices: 78.1 us -> 31.5 us  [body(): lax.all_gather(up_weight, 'fsdp', axis=0, tiled=True)]
    unnamed x139 -> x174, local copies, waits for them, and re-layouts: 12.2 us -> 37.3 us
  transfers between devices with their start and end apart: 20 -> 26, of which waited for: 18 -> 22; matrix products, arithmetic and copies ran while one was open for 20% -> 23% of each run, Pallas kernels for 0% -> 0%
where the time goes in v1:
time: 1390 us; the launch traced here: 1380 us
  waiting for transfers between devices  881 us (63%)
  matrix products  278 us (20%)
  other arithmetic  82.6 us (6%)
  blocking collectives  79.7 us (6%)
  local copies, waits for them, and re-layouts  42.2 us (3%)
  between operations  15.8 us (1%)
    reduce_scatter x4, waiting for transfers between devices, scatter_rows(): return lax.psum_scatter(partial_sums, 'tp', scatter_dimension=0, tiled=True)  320 us
    ppermute x7, waiting for transfers between devices, body(): lax.ppermute(ring[-1], 'fsdp', [(dev, (dev + 1) % 8) for dev in range(8)])  169 us
    reduce_scatter x1, waiting for transfers between devices, body(): lax.psum_scatter(down_grad.astype(jnp.bfloat16), 'fsdp', scatter_dimensio...  87.4 us
    dot_general x11, matrix products, times_transposed(): lax.dot_general(left, right, (((1,), (1,)), ((), ())), preferred_element_...  69.9 us
    reduce_scatter x1, waiting for transfers between devices, body(): lax.psum_scatter(up_grad.astype(jnp.bfloat16), 'fsdp', scatter_dimension=...  59.9 us
    dot_general x7, matrix products, contract_rows(): lax.dot_general(left, right, (((0,), (0,)), ((), ())), preferred_element_...  57.9 us
    all_gather x4, waiting for transfers between devices, gather_rows(): return lax.all_gather(pieces, 'tp', axis=0, tiled=True)  54.3 us
    unnamed x174, local copies, waits for them, and re-layouts  37.3 us
  transfers between devices with their start and end apart: 26, of which 22 were waited for; matrix products, arithmetic and copies ran while one was open for 23% of the time, Pallas kernels for 0%

profile of v1, /device:TPU:0, one launch (start us, length us, event | category | flops | bytes accessed | tf_op | source)
XLA Modules:
  0.0 1380.6 jit_solution(16854346098355403065)
XLA Ops:
  10.0 13.4 all-gather
  34.1 14.9 %all_gather.39 = bf16[2048,128]{1,0:T(8,128)(2,1)S(1)} all-gather(bf16[256,128]{1,0:T(8,128)(2,1)S(1)} %copy-done.47), channel_id=1, replica_groups=mesh['fsdp'=8,'tp'=4] {'fsdp'}, dimensions={0}, use_global_device_ids=true | all-gather | bytes 589824 | tf_op jit(solution)/shard_map/all_gather | solution.py:114
  52.4 15.0 %all_gather.38 = bf16[2048,128]{1,0:T(8,128)(2,1)S(1)} all-gather(bf16[256,128]{1,0:T(8,128)(2,1)S(1)} %copy-done.48), channel_id=1, replica_groups=mesh['fsdp'=8,'tp'=4] {'fsdp'}, dimensions={0}, use_global_device_ids=true | all-gather | bytes 589824 | tf_op jit(solution)/shard_map/all_gather | solution.py:115
  81.4 27.0 %all-gather.13.cloned.1.call-done = bf16[2048,512]{1,0:T(8,128)(2,1)} async-done(((bf16[256,512]{1,0:T(8,128)(2,1)}), bf16[2048,512]{1,0:T(8,128)(2,1)}) %all-gather.13.cloned.1.call-update) | async-done | bytes 2097168 | tf_op jit(solution)/shard_map/all_gather | solution.py:113
  116.5 7.3 fusion.92
  123.8 8.4 fusion.6
  133.8 7.7 fusion.46
  141.5 7.8 fusion.91
  149.3 8.1 fusion.7
  158.0 7.4 fusion.45
  165.5 7.5 fusion.61
  173.6 10.4 all-gather.1
  184.0 75.0 %reduce-scatter.12.cloned.1.call-done = f32[256,2048]{1,0:T(8,128)} async-done(((f32[1024,2048]{1,0:T(8,128)}), f32[256,2048]{1,0:T(8,128)}) %reduce-scatter.12.cloned.1.call-update) | async-done | bytes 2097168 | tf_op jit(solution)/shard_map/reduce_scatter | solution.py:74
  263.1 28.0 %collective-permute-done = bf16[2048,256]{1,0:T(8,128)(2,1)S(1)} collective-permute-done((bf16[2048,256]{1,0:T(8,128)(2,1)}, bf16[2048,256]{1,0:T(8,128)(2,1)S(1)}, u32[]{:S(2)}, u32[]{:S(2)}) %collective-permute-start) | collective-permute-done | bytes 1048608 | tf_op jit(solution)/shard_map/ppermute | solution.py:167
  292.1 38.5 %collective-permute-done.1 = bf16[2048,256]{1,0:T(8,128)(2,1)S(1)} collective-permute-done((bf16[2048,256]{1,0:T(8,128)(2,1)S(1)}, bf16[2048,256]{1,0:T(8,128)(2,1)S(1)}, u32[]{:S(2)}, u32[]{:S(2)}) %collective-permute-start.1) | collective-permute-done | bytes 1048608 | tf_op jit(solution)/shard_map/ppermute | solution.py:167
  331.6 37.8 %collective-permute-done.2 = bf16[2048,256]{1,0:T(8,128)(2,1)S(1)} collective-permute-done((bf16[2048,256]{1,0:T(8,128)(2,1)S(1)}, bf16[2048,256]{1,0:T(8,128)(2,1)S(1)}, u32[]{:S(2)}, u32[]{:S(2)}) %collective-permute-start.2) | collective-permute-done | bytes 1048608 | tf_op jit(solution)/shard_map/ppermute | solution.py:167
  370.3 16.0 %collective-permute-done.3 = bf16[2048,256]{1,0:T(8,128)(2,1)S(1)} collective-permute-done((bf16[2048,256]{1,0:T(8,128)(2,1)S(1)}, bf16[2048,256]{1,0:T(8,128)(2,1)S(1)}, u32[]{:S(2)}, u32[]{:S(2)}) %collective-permute-start.3) | collective-permute-done | bytes 1048608 | tf_op jit(solution)/shard_map/ppermute | solution.py:167
  387.3 16.0 %collective-permute-done.4 = bf16[2048,256]{1,0:T(8,128)(2,1)S(1)} collective-permute-done((bf16[2048,256]{1,0:T(8,128)(2,1)S(1)}, bf16[2048,256]{1,0:T(8,128)(2,1)S(1)}, u32[]{:S(2)}, u32[]{:S(2)}) %collective-permute-start.4) | collective-permute-done | bytes 1048608 | tf_op jit(solution)/shard_map/ppermute | solution.py:167
  404.3 16.1 %collective-permute-done.5 = bf16[2048,256]{1,0:T(8,128)(2,1)} collective-permute-done((bf16[2048,256]{1,0:T(8,128)(2,1)S(1)}, bf16[2048,256]{1,0:T(8,128)(2,1)}, u32[]{:S(2)}, u32[]{:S(2)}) %collective-permute-start.5) | collective-permute-done | bytes 1048608 | tf_op jit(solution)/shard_map/ppermute | solution.py:167
  420.6 16.2 %collective-permute-done.6 = bf16[2048,256]{1,0:T(8,128)(2,1)} collective-permute-done((bf16[2048,256]{1,0:T(8,128)(2,1)}, bf16[2048,256]{1,0:T(8,128)(2,1)}, u32[]{:S(2)}, u32[]{:S(2)}) %collective-permute-start.6) | collective-permute-done | bytes 1048608 | tf_op jit(solution)/shard_map/ppermute | solution.py:167
  461.9 14.7 %fusion.95 = f32[1024,2048]{1,0:T(8,128)} fusion(bf16[1024,2048]{1,0:T(8,128)(2,1)} %all-gather.17.cloned.1.call-done, bf16[2048,2048]{1,0:T(8,128)(2,1)} %all-gather.19.cloned.1.call-done), kind=kOutput, calls=%fused_computation.176 | convolution fusion | flops 8589934592 | bytes 20971520 | tf_op jit(solution)/shard_map/dot_general | solution.py:174
  476.6 31.5 %all-gather.21.cloned.1.call-done = bf16[2048,2048]{1,0:T(8,128)(2,1)} async-done(((bf16[256,2048]{1,0:T(8,128)(2,1)}), bf16[2048,2048]{1,0:T(8,128)(2,1)}) %all-gather.21.cloned.1.call-update) | async-done | bytes 8388624 | tf_op jit(solution)/shard_map/all_gather | solution.py:162
  508.1 14.4 %fusion.96 = f32[1024,2048]{1,0:T(8,128)} fusion(bf16[1024,2048]{1,0:T(8,128)(2,1)} %all-gather.17.cloned.1.call-done, bf16[2048,2048]{1,0:T(8,128)(2,1)} %all-gather.21.cloned.1.call-done), kind=kOutput, calls=%fused_computation.177 | convolution fusion | flops 8589934592 | bytes 20971520 | tf_op jit(solution)/shard_map/dot_general | solution.py:175
  522.5 38.8 %all-gather.23.cloned.1.call-done = bf16[1024,2048]{1,0:T(8,128)(2,1)} async-done(((bf16[256,2048]{1,0:T(8,128)(2,1)}), bf16[1024,2048]{1,0:T(8,128)(2,1)}) %all-gather.23.cloned.1.call-update) | async-done | bytes 4194320 | tf_op jit(solution)/shard_map/all_gather | solution.py:70
  561.3 21.9 %fusion.18 = (bf16[1024,2048]{1,0:T(8,128)(2,1)}, bf16[1024,2048]{1,0:T(8,128)(2,1)}, bf16[1024,2048]{1,0:T(8,128)(2,1)}) fusion(f32[1024,2048]{1,0:T(8,128)} %fusion.95, f32[1024,2048]{1,0:T(8,128)} %fusion.96, bf16[1024,2048]{1,0:T(8,128)(2,1)} %all-gather.23.cloned.1.call-done, bf16[2048,4096]{1,0:T(8,128)(2,1)} %constant_dynamic-update-slice_fusion, ...), kind=kOutput, calls=%fused_computation.30 | convolution fusion | flops 8623489024 | bytes 41943044 | tf_op jit(solution)/shard_map/dot_general | solution.py:64
  583.2 14.8 %fusion.97 = f32[1024,2048]{1,0:T(8,128)} fusion(bf16[1024,2048]{1,0:T(8,128)(2,1)} %get-tuple-element.24, bf16[2048,2048]{1,0:T(8,128)(2,1)} %all-gather.19.cloned.1.call-done), kind=kOutput, calls=%fused_computation.178 | convolution fusion | flops 8589934592 | bytes 20971520 | tf_op jit(solution)/shard_map/dot_general | solution.py:64
  598.0 13.0 convolution_add_fusion
  611.1 14.4 %fusion.25 = f32[1024,2048]{1,0:T(8,128)} fusion(bf16[1024,2048]{1,0:T(8,128)(2,1)} %get-tuple-element.25, bf16[2048,4096]{1,0:T(8,128)(2,1)} %constant_dynamic-update-slice_fusion, s32[]{:T(128)S(6)} %select_n.25), kind=kOutput, calls=%fused_computation.43 | convolution fusion | flops 8589934592 | bytes 20971524 | tf_op jit(solution)/shard_map/dot_general | solution.py:179
  625.6 72.0 %reduce-scatter.16.cloned.1.call-done = f32[256,2048]{1,0:T(8,128)} async-done(((f32[1024,2048]{1,0:T(8,128)}), f32[256,2048]{1,0:T(8,128)}) %reduce-scatter.16.cloned.1.call-update) | async-done | bytes 2097168 | tf_op jit(solution)/shard_map/reduce_scatter | solution.py:74
  700.3 86.6 %reduce-scatter.14.cloned.1.call-done = f32[256,2048]{1,0:T(8,128)} async-done(((f32[1024,2048]{1,0:T(8,128)}), f32[256,2048]{1,0:T(8,128)}) %reduce-scatter.14.cloned.1.call-update) | async-done | bytes 2097168 | tf_op jit(solution)/shard_map/reduce_scatter | solution.py:74
  792.0 14.5 %convolution_convert_fusion.2 = bf16[2048,2048]{1,0:T(8,128)(2,1)} fusion(bf16[1024,2048]{1,0:T(8,128)(2,1)} %all-gather.17.cloned.1.call-done, bf16[1024,2048]{1,0:T(8,128)(2,1)} %get-tuple-element.24), kind=kOutput, calls=%fused_computation.40 | convolution fusion | flops 8594128896 | bytes 16777216 | tf_op jit(solution)/shard_map/dot_general | solution.py:58
  806.5 14.1 %convolution_convert_fusion.1 = bf16[2048,2048]{1,0:T(8,128)(2,1)} fusion(bf16[1024,2048]{1,0:T(8,128)(2,1)} %all-gather.17.cloned.1.call-done, bf16[1024,2048]{1,0:T(8,128)(2,1)} %get-tuple-element.23), kind=kOutput, calls=%fused_computation.39 | convolution fusion | flops 8594128896 | bytes 16777216 | tf_op jit(solution)/shard_map/dot_general | solution.py:58
  820.7 14.3 %convolution_convert_fusion = bf16[2048,2048]{1,0:T(8,128)(2,1)} fusion(bf16[1024,2048]{1,0:T(8,128)(2,1)} %get-tuple-element.25, bf16[1024,2048]{1,0:T(8,128)(2,1)} %all-gather.23.cloned.1.call-done), kind=kOutput, calls=%fused_computation.38 | convolution fusion | flops 8594128896 | bytes 16777216 | tf_op jit(solution)/shard_map/dot_general | solution.py:58
  835.8 9.0 all-gather.25.cloned.1.call-done
  850.4 10.7 fusion.47
  869.3 15.1 %fusion = (f32[2,4,512]{2,1,0:T(4,128)S(1)}, f32[2,1024,512,4]{2,1,3,0:T(8,128)}) fusion(f32[2,4,512,1024]{2,3,1,0:T(8,128)} %get-tuple-element.48, f32[2,4,512]{2,1,0:T(4,128)S(1)} %bitcast.200, bf16[1024,2,64,1]{0,2,3,1:T(8,128)(2,1)} %bitcast.190, bf16[512,2,4,64]{0,3,2,1:T(8,128)(2,1)} %bitcast.181), kind=kOutput, calls=%fused_computation.2 | convolution fusion | flops 549449728 | bytes 34373632 | tf_op jit(solution)/shard_map/qkgd,skd->kgqs/dot_general | solution.py:217
  884.4 12.3 fusion.2
  902.8 7.6 fusion.3
  910.4 10.8 fusion.5
  967.2 59.9 %reduce-scatter.30.cloned.1.call-done = bf16[256,2048]{1,0:T(8,128)(2,1)} async-done(((bf16[2048,2048]{1,0:T(8,128)(2,1)}), bf16[256,2048]{1,0:T(8,128)(2,1)}) %reduce-scatter.30.cloned.1.call-update) | async-done | bytes 1048592 | tf_op jit(solution)/shard_map/reduce_scatter | solution.py:277
  1029.9 87.4 %reduce-scatter.32.cloned.1.call-done = bf16[2048,256]{1,0:T(8,128)(2,1)} async-done(((bf16[2048,2048]{1,0:T(8,128)(2,1)}), bf16[2048,256]{1,0:T(8,128)(2,1)}) %reduce-scatter.32.cloned.1.call-update) | async-done | bytes 1048592 | tf_op jit(solution)/shard_map/reduce_scatter | solution.py:285
  1120.0 28.9 %reduce-scatter.24.cloned.1.call-done = bf16[256,128]{1,0:T(8,128)(2,1)} async-done(((bf16[2048,128]{1,0:T(8,128)(2,1)}), bf16[256,128]{1,0:T(8,128)(2,1)}) %reduce-scatter.24.cloned.1.call-update) | async-done | bytes 65552 | tf_op jit(solution)/shard_map/reduce_scatter | solution.py:268
  1150.4 30.3 %reduce-scatter.22.cloned.1.call-done = bf16[256,128]{1,0:T(8,128)(2,1)} async-done(((bf16[2048,128]{1,0:T(8,128)(2,1)}), bf16[256,128]{1,0:T(8,128)(2,1)}) %reduce-scatter.22.cloned.1.call-update) | async-done | bytes 65552 | tf_op jit(solution)/shard_map/reduce_scatter | solution.py:265
  1182.2 34.9 %reduce-scatter.26.cloned.1.call-done = bf16[512,256]{1,0:T(8,128)(2,1)} async-done(((bf16[512,2048]{1,0:T(8,128)(2,1)}), bf16[512,256]{1,0:T(8,128)(2,1)}) %reduce-scatter.26.cloned.1.call-update) | async-done | bytes 262160 | tf_op jit(solution)/shard_map/reduce_scatter | solution.py:282
  1218.9 34.9 %reduce-scatter.20.cloned.1.call-done = bf16[256,512]{1,0:T(8,128)(2,1)} async-done(((bf16[2048,512]{1,0:T(8,128)(2,1)}), bf16[256,512]{1,0:T(8,128)(2,1)}) %reduce-scatter.20.cloned.1.call-update) | async-done | bytes 262160 | tf_op jit(solution)/shard_map/reduce_scatter | solution.py:262
  1255.6 86.5 %reduce-scatter.18.cloned.1.call-done = f32[256,2048]{1,0:T(8,128)} async-done(((f32[1024,2048]{1,0:T(8,128)}), f32[256,2048]{1,0:T(8,128)}) %reduce-scatter.18.cloned.1.call-update) | async-done | bytes 2097168 | tf_op jit(solution)/shard_map/reduce_scatter | solution.py:74
  1344.3 16.6 %all-reduce.3 = (bf16[2048]{0:T(1024)(128)(2,1)S(1)}, bf16[2048]{0:T(1024)(128)(2,1)S(1)}) all-reduce(bf16[2048]{0:T(1024)(128)(2,1)S(1)} %get-tuple-element.13, bf16[2048]{0:T(1024)(128)(2,1)S(1)} %copy-done.56), channel_id=6, replica_groups=mesh['fsdp'=8,'tp'=4] {'fsdp'}, use_global_device_ids=true, to_apply=%region_15.16.clone | all-reduce | flops 4096 | bytes 16384
  1360.9 9.5 all-reduce.2
  (294 shorter events, 167.0 us)
Async XLA Ops:
  7.2 41.8 %copy-start.59 = (f32[32]{0:T(128)S(1)}, f32[32]{0:T(128)}, u32[]{:S(2)}) copy-start(f32[32]{0:T(128)} %constant.58.clone) | copy-start | bytes 388
  7.2 43.6 %copy-start.53 = (s32[1024]{0:T(1024)S(1)}, s32[1024]{0:T(1024)}, u32[]{:S(2)}) copy-start(s32[1024]{0:T(1024)} %param.17) | copy-start | bytes 12292
  7.2 26.8 %copy-start.47 = (bf16[256,128]{1,0:T(8,128)(2,1)S(1)}, bf16[256,128]{1,0:T(8,128)(2,1)}, u32[]{:S(2)}) copy-start(bf16[256,128]{1,0:T(8,128)(2,1)} %param.22) | copy-start | bytes 196612
  7.2 41.7 %copy-start.58 = (s32[1024]{0:T(1024)S(1)}, s32[1024]{0:T(1024)}, u32[]{:S(2)}) copy-start(s32[1024]{0:T(1024)} %param.18) | copy-start | bytes 12292
  7.2 70.4 %all-gather.11.cloned.1.call-start = ((), (), s32[]{:S(2)}) async-start(), calls=%async_computation.11 | async-start | bytes 5242880 | tf_op jit(solution)/shard_map/all_gather | solution.py:70
  9.3 43.0 %copy-start.54 = (f32[256]{0:T(256)}, f32[256]{0:T(256)S(1)}, u32[]{:S(2)}) copy-start(f32[256]{0:T(256)S(1)} %get-tuple-element.44) | copy-start | bytes 3076
  24.0 28.4 %copy-start.48 = (bf16[256,128]{1,0:T(8,128)(2,1)S(1)}, bf16[256,128]{1,0:T(8,128)(2,1)}, u32[]{:S(2)}) copy-start(bf16[256,128]{1,0:T(8,128)(2,1)} %param.23) | copy-start | bytes 196612
  26.6 81.8 %all-gather.13.cloned.1.call-start = ((), (), s32[]{:S(2)}) async-start(), calls=%async_computation.12 | async-start | bytes 2359296 | tf_op jit(solution)/shard_map/all_gather | solution.py:113
  27.3 138.1 %all-gather.15.cloned.1.call-start = ((), (), s32[]{:S(2)}) async-start(), calls=%async_computation.13 | async-start | bytes 2359296 | tf_op jit(solution)/shard_map/all_gather | solution.py:156
  28.1 230.9 %reduce-scatter.12.cloned.1.call-start = ((), (), s32[]{:S(2)}) async-start(), calls=%async_computation.14 | async-start | bytes 10485760 | tf_op jit(solution)/shard_map/reduce_scatter | solution.py:74
  49.0 32.4 %copy-start.12 = (bf16[2048,128]{1,0:T(8,128)(2,1)}, bf16[2048,128]{1,0:T(8,128)(2,1)S(1)}, u32[]{:S(2)}) copy-start(bf16[2048,128]{1,0:T(8,128)(2,1)S(1)} %all_gather.39) | copy-start | bytes 1572868
  50.7 63.1 %copy-start.34 = (f32[1024,64]{0,1:T(8,128)}, f32[1024,64]{0,1:T(8,128)S(1)}, u32[]{:S(2)}) copy-start(f32[1024,64]{0,1:T(8,128)S(1)} %get-tuple-element.42) | copy-start | bytes 786436
  50.7 64.5 %copy-start.21 = (f32[1024,64]{0,1:T(8,128)}, f32[1024,64]{0,1:T(8,128)S(1)}, u32[]{:S(2)}) copy-start(f32[1024,64]{0,1:T(8,128)S(1)} %get-tuple-element.41) | copy-start | bytes 786436
  67.4 64.8 %copy-start.14 = (bf16[2048,128]{1,0:T(8,128)(2,1)}, bf16[2048,128]{1,0:T(8,128)(2,1)S(1)}, u32[]{:S(2)}) copy-start(bf16[2048,128]{1,0:T(8,128)(2,1)S(1)} %all_gather.38) | copy-start | bytes 1572868
  165.4 93.5 %copy-start.1 = (bf16[256,2048]{1,0:T(8,128)(2,1)S(1)}, bf16[256,2048]{1,0:T(8,128)(2,1)}, u32[]{:S(2)}) copy-start(bf16[256,2048]{1,0:T(8,128)(2,1)} %param.15) | copy-start | bytes 3145732
  172.9 288.9 %all-gather.19.cloned.1.call-start = ((), (), s32[]{:S(2)}) async-start(), calls=%async_computation.16 | async-start | bytes 9437184 | tf_op jit(solution)/shard_map/all_gather | solution.py:161
  173.5 288.3 %all-gather.17.cloned.1.call-start = ((), (), s32[]{:S(2)}) async-start(), calls=%async_computation.15 | async-start | bytes 5242880 | tf_op jit(solution)/shard_map/all_gather | solution.py:70
  262.2 187.3 %copy-start.23 = (bf16[2048,256]{1,0:T(8,128)(2,1)S(1)}, bf16[2048,256]{1,0:T(8,128)(2,1)}, u32[]{:S(2)}) copy-start(bf16[2048,256]{1,0:T(8,128)(2,1)} %param.28) | copy-start | bytes 3145732
  262.2 245.9 %all-gather.21.cloned.1.call-start = ((), (), s32[]{:S(2)}) async-start(), calls=%async_computation.17 | async-start | bytes 9437184 | tf_op jit(solution)/shard_map/all_gather | solution.py:162
  262.9 298.4 %all-gather.23.cloned.1.call-start = ((), (), s32[]{:S(2)}) async-start(), calls=%async_computation.19 | async-start | bytes 5242880 | tf_op jit(solution)/shard_map/all_gather | solution.py:70
  263.0 28.1 %collective-permute-start = (bf16[2048,256]{1,0:T(8,128)(2,1)}, bf16[2048,256]{1,0:T(8,128)(2,1)S(1)}, u32[]{:S(2)}, u32[]{:S(2)}) collective-permute-start(bf16[2048,256]{1,0:T(8,128)(2,1)} %param.28), channel_id=1, source_target_pairs={{0,4},{4,8},{8,12},{12,16},{16,20},{20,24},{24,28},{28,0},{1,5},{5... | collective-permute-start | bytes 3145736 | tf_op jit(solution)/shard_map/ppermute | solution.py:167
  292.1 38.5 %collective-permute-start.1 = (bf16[2048,256]{1,0:T(8,128)(2,1)S(1)}, bf16[2048,256]{1,0:T(8,128)(2,1)S(1)}, u32[]{:S(2)}, u32[]{:S(2)}) collective-permute-start(bf16[2048,256]{1,0:T(8,128)(2,1)S(1)} %collective-permute-done), channel_id=1, source_target_pairs={{0,4},{4,8},{8,12},{12,16},{16,20},{20,24},{24,28},{28,0},{1,5},{5... | collective-permute-start | bytes 3145736 | tf_op jit(solution)/shard_map/ppermute | solution.py:167
  331.6 37.8 %collective-permute-start.2 = (bf16[2048,256]{1,0:T(8,128)(2,1)S(1)}, bf16[2048,256]{1,0:T(8,128)(2,1)S(1)}, u32[]{:S(2)}, u32[]{:S(2)}) collective-permute-start(bf16[2048,256]{1,0:T(8,128)(2,1)S(1)} %collective-permute-done.1), channel_id=1, source_target_pairs={{0,4},{4,8},{8,12},{12,16},{16,20},{20,24},{24,28},{28,0},{1,5},{5... | collective-permute-start | bytes 3145736 | tf_op jit(solution)/shard_map/ppermute | solution.py:167
  370.3 16.0 %collective-permute-start.3 = (bf16[2048,256]{1,0:T(8,128)(2,1)S(1)}, bf16[2048,256]{1,0:T(8,128)(2,1)S(1)}, u32[]{:S(2)}, u32[]{:S(2)}) collective-permute-start(bf16[2048,256]{1,0:T(8,128)(2,1)S(1)} %collective-permute-done.2), channel_id=1, source_target_pairs={{0,4},{4,8},{8,12},{12,16},{16,20},{20,24},{24,28},{28,0},{1,5},{5... | collective-permute-start | bytes 3145736 | tf_op jit(solution)/shard_map/ppermute | solution.py:167
  387.3 16.0 %collective-permute-start.4 = (bf16[2048,256]{1,0:T(8,128)(2,1)S(1)}, bf16[2048,256]{1,0:T(8,128)(2,1)S(1)}, u32[]{:S(2)}, u32[]{:S(2)}) collective-permute-start(bf16[2048,256]{1,0:T(8,128)(2,1)S(1)} %collective-permute-done.3), channel_id=1, source_target_pairs={{0,4},{4,8},{8,12},{12,16},{16,20},{20,24},{24,28},{28,0},{1,5},{5... | collective-permute-start | bytes 3145736 | tf_op jit(solution)/shard_map/ppermute | solution.py:167
  404.3 16.1 %collective-permute-start.5 = (bf16[2048,256]{1,0:T(8,128)(2,1)S(1)}, bf16[2048,256]{1,0:T(8,128)(2,1)}, u32[]{:S(2)}, u32[]{:S(2)}) collective-permute-start(bf16[2048,256]{1,0:T(8,128)(2,1)S(1)} %collective-permute-done.4), channel_id=1, source_target_pairs={{0,4},{4,8},{8,12},{12,16},{16,20},{20,24},{24,28},{28,0},{1,5},{5... | collective-permute-start | bytes 3145736 | tf_op jit(solution)/shard_map/ppermute | solution.py:167
  420.4 16.3 %collective-permute-start.6 = (bf16[2048,256]{1,0:T(8,128)(2,1)}, bf16[2048,256]{1,0:T(8,128)(2,1)}, u32[]{:S(2)}, u32[]{:S(2)}) collective-permute-start(bf16[2048,256]{1,0:T(8,128)(2,1)} %collective-permute-done.5), channel_id=1, source_target_pairs={{0,4},{4,8},{8,12},{12,16},{16,20},{20,24},{24,28},{28,0},{1,5},{5... | collective-permute-start | bytes 3145736 | tf_op jit(solution)/shard_map/ppermute | solution.py:167
  420.4 277.2 %reduce-scatter.16.cloned.1.call-start = ((), (), s32[]{:S(2)}) async-start(), calls=%async_computation.20 | async-start | bytes 10485760 | tf_op jit(solution)/shard_map/reduce_scatter | solution.py:74
  420.5 27.9 %copy-start.25 = (bf16[2048,256]{1,0:T(8,128)(2,1)S(1)}, bf16[2048,256]{1,0:T(8,128)(2,1)}, u32[]{:S(2)}) copy-start(bf16[2048,256]{1,0:T(8,128)(2,1)} %copy-done.24) | copy-start | bytes 3145732
  611.1 175.9 %reduce-scatter.14.cloned.1.call-start = ((), (), s32[]{:S(2)}) async-start(), calls=%async_computation.18 | async-start | bytes 10485760 | tf_op jit(solution)/shard_map/reduce_scatter | solution.py:74
  625.5 161.4 %copy-start.20 = (bf16[256,2048]{1,0:T(8,128)(2,1)S(1)}, bf16[256,2048]{1,0:T(8,128)(2,1)}, u32[]{:S(2)}) copy-start(bf16[256,2048]{1,0:T(8,128)(2,1)} %param.16) | copy-start | bytes 3145732
  625.5 219.3 %all-gather.25.cloned.1.call-start = ((), (), s32[]{:S(2)}) async-start(), calls=%async_computation.21 | async-start | bytes 5242880 | tf_op jit(solution)/shard_map/all_gather | solution.py:70
  792.0 172.4 %reduce-scatter.28.cloned.1.call-start = ((), (), s32[]{:S(2)}) async-start(), calls=%async_computation.27 | async-start | bytes 9437184 | tf_op jit(solution)/shard_map/reduce_scatter | solution.py:274
  806.5 220.6 %reduce-scatter.30.cloned.1.call-start = ((), (), s32[]{:S(2)}) async-start(), calls=%async_computation.28 | async-start | bytes 9437184 | tf_op jit(solution)/shard_map/reduce_scatter | solution.py:277
  820.7 296.7 %reduce-scatter.32.cloned.1.call-start = ((), (), s32[]{:S(2)}) async-start(), calls=%async_computation.29 | async-start | bytes 9437184 | tf_op jit(solution)/shard_map/reduce_scatter | solution.py:285
  835.1 313.8 %reduce-scatter.24.cloned.1.call-start = ((), (), s32[]{:S(2)}) async-start(), calls=%async_computation.25 | async-start | bytes 589824 | tf_op jit(solution)/shard_map/reduce_scatter | solution.py:268
  869.3 33.5 %slice-start = ((s8[16777216]{0:T(1024)(128)(4,1)}), s8[4194304]{0:T(1024)(128)(4,1)S(1)}, s32[]{:S(2)}) async-start(s8[16777216]{0:T(1024)(128)(4,1)} %bitcast.172), calls=%async_computation.30 | async-start | bytes 8388608
  869.3 33.5 %slice-start.1 = ((s8[16777216]{0:T(1024)(128)(4,1)}), s8[4194304]{0:T(1024)(128)(4,1)S(1)}, s32[]{:S(2)}) async-start(s8[16777216]{0:T(1024)(128)(4,1)} %bitcast.172), calls=%async_computation.31 | async-start | bytes 8388608
  921.2 259.5 %reduce-scatter.22.cloned.1.call-start = ((), (), s32[]{:S(2)}) async-start(), calls=%async_computation.24 | async-start | bytes 589824 | tf_op jit(solution)/shard_map/reduce_scatter | solution.py:265
  930.3 286.8 %reduce-scatter.26.cloned.1.call-start = ((), (), s32[]{:S(2)}) async-start(), calls=%async_computation.26 | async-start | bytes 2359296 | tf_op jit(solution)/shard_map/reduce_scatter | solution.py:282
  936.3 317.5 %reduce-scatter.20.cloned.1.call-start = ((), (), s32[]{:S(2)}) async-start(), calls=%async_computation.23 | async-start | bytes 2359296 | tf_op jit(solution)/shard_map/reduce_scatter | solution.py:262
  953.5 388.6 %reduce-scatter.18.cloned.1.call-start = ((), (), s32[]{:S(2)}) async-start(), calls=%async_computation.22 | async-start | bytes 10485760 | tf_op jit(solution)/shard_map/reduce_scatter | solution.py:74
  962.5 379.6 %copy-start.2 = (bf16[256,2048]{1,0:T(8,128)(2,1)S(1)}, bf16[256,2048]{1,0:T(8,128)(2,1)}, u32[]{:S(2)}) copy-start(bf16[256,2048]{1,0:T(8,128)(2,1)} %param.15) | copy-start | bytes 3145732
  962.5 379.6 %copy-start.46 = (f32[8,1,256]{2,1,0:T(1,128)S(1)}, f32[8,1,256]{2,1,0:T(1,128)}, u32[]{:S(2)}) copy-start(f32[8,1,256]{2,1,0:T(1,128)} %copy-done.45) | copy-start | bytes 24580
  962.5 379.6 %copy-start.55 = (f32[256]{0:T(256)S(1)}, f32[256]{0:T(256)}, u32[]{:S(2)}) copy-start(f32[256]{0:T(256)} %copy-done.54) | copy-start | bytes 3076
  962.5 381.7 %copy-start.56 = (bf16[2048]{0:T(1024)(128)(2,1)S(1)}, bf16[2048]{0:T(1024)(128)(2,1)}, u32[]{:S(2)}) copy-start(bf16[2048]{0:T(1024)(128)(2,1)} %get-tuple-element.11) | copy-start | bytes 12292
  962.5 407.9 %copy-start.7 = (f32[256,2048]{1,0:T(8,128)S(1)}, f32[256,2048]{1,0:T(8,128)}, u32[]{:S(2)}) copy-start(f32[256,2048]{1,0:T(8,128)} %get-tuple-element.20) | copy-start | bytes 6291460
  962.5 407.8 %copy-start.57 = (f32[256]{0:T(256)S(1)}, f32[256]{0:T(256)}, u32[]{:S(2)}) copy-start(f32[256]{0:T(256)} %get-tuple-element.43) | copy-start | bytes 3076
  (56 other events, 479.2 us)
Sparse Core Ops, SparseCore 0:
  26.7 50.9 all-gather.10
  79.3 29.0 all-gather.12
  110.0 30.3 all-gather.14
  173.1 85.8 reduce-scatter.11
  260.5 110.0 all-gather.18
  373.0 51.2 all-gather.16
  426.0 82.0 all-gather.20
  510.0 51.2 all-gather.22
  611.2 86.4 reduce-scatter.15
  700.5 86.3 reduce-scatter.13
  792.1 52.6 all-gather.24
  847.1 89.5 reduce-scatter.27
  939.1 87.9 reduce-scatter.29
  1029.4 87.9 reduce-scatter.31
  1119.5 29.3 reduce-scatter.23
  1151.6 29.0 reduce-scatter.21
  1183.0 34.0 reduce-scatter.25
  1219.3 34.4 reduce-scatter.19
  1257.2 84.8 reduce-scatter.17
